TPU v7x, 32 devices: a whole 2x2x4 slice. The times are simulated.
32 devices in a mesh: spec: 4 (over y, x), space: 8 (over z, core).
Axes of the slice: x: 2, y: 2, z: 4, core: 2. Of those that a mesh axis runs over, the one named last changes fastest.
Arguments:
- spectrum: float32 [1296, 32, 1024], P('spec', 'space'), may hold values from 0.05 to 2
- wind: float32 [2, 32, 1024], P(None, 'space'), may hold values from -5 to 5
- courant: float32 [2, 1296], P(None, 'spec'), may hold values from -0.5 to 0.5
- transfer: bfloat16 [1296, 1296], replicated
- sea_cells: int32 [8, 1920], P('space'), may hold values from 0 to 4095, as said below
Outputs:
- spectrum_out: float32 [1296, 32, 1024], P('spec', 'space')
Inputs may be any that keep to these rules, and one draw needn't show every extreme that they name: `sea_cells`: each row lists the 1920 sea cells of one slab in ascending order, each once. Cut a slab's 4 * 1024 flattened cells into 4 aligned tiles of 1024 cells: a quarter of the tiles hold 1024 sea cells, a quarter 1024 // 2, a quarter 1024 // 4 and a quarter 1024 // 8, in an order drawn from the seed; the sea cells of a tile are its first ones.
All inputs are finite; a program needn't handle non-finite values.
Results may differ from a plain program's by a relative error of at most 0.0011.
Values sent between devices are 32-bit elements; how exact they have to be, the bound alone decides.
A program may use at most 128 MiB of HBM per device.

v0:
```python
import math

import jax
import jax.numpy as jnp
from jax import lax
from jax.sharding import PartitionSpec as P

NDIR = 36
NFREQ = 36
SUB = 4
SRC_STEPS = 4


growth_rate = 0.05
whitecap = 0.1


def padded_2(cells, sides, width):
    for axis, dim in sides:
        count = lax.axis_size(axis)
        ends = count - 1
        head = lax.slice_in_dim(cells, 0, width, axis=dim)
        tail = lax.slice_in_dim(cells, cells.shape[dim] - width, cells.shape[dim], axis=dim)
        cells = jnp.concatenate(
            [
                lax.ppermute(tail, axis, [(i, (i + 1) % count) for i in range(ends)]),
                cells,
                lax.ppermute(head, axis, [((i + 1) % count, i) for i in range(ends)]),
            ],
            axis=dim,
        )
    return cells


def source_terms(points, wind_pts, transfer):
    angle = jnp.arange(NDIR, dtype=jnp.float32) * (2.0 * math.pi / NDIR)
    cos_comp = jnp.repeat(jnp.cos(angle), NFREQ)
    sin_comp = jnp.repeat(jnp.sin(angle), NFREQ)
    growth = jnp.tile(growth_rate * (jnp.arange(NFREQ, dtype=jnp.float32) + 1.0) / NFREQ, NDIR)
    drive = jnp.maximum(
        cos_comp[:, None] * wind_pts[0][None, :] + sin_comp[:, None] * wind_pts[1][None, :], 0.0
    )
    gamma = growth[:, None] * drive
    for step in range(SRC_STEPS):
        low = points.astype(jnp.bfloat16)
        moved = jnp.dot(transfer, low, preferred_element_type=jnp.float32)
        mean = jnp.mean(points, axis=0, keepdims=True)
        points = points + (gamma - whitecap * mean) * points + moved
    return points


def advance(padded, cx, cy):
    centre = padded[:, 1:-1]
    upper = padded[:, :-2]
    lower = padded[:, 2:]
    left = jnp.roll(centre, 1, axis=2)
    right = jnp.roll(centre, -1, axis=2)
    return (
        centre
        - jnp.maximum(cx, 0.0) * (centre - upper)
        - jnp.minimum(cx, 0.0) * (lower - centre)
        - jnp.maximum(cy, 0.0) * (centre - left)
        - jnp.minimum(cy, 0.0) * (right - centre)
    )


def body(spectrum, wind, courant, transfer, sea_cells):
    comps, rows, cols = spectrum.shape
    cells = rows * cols
    groups = lax.axis_size("spec")
    member = lax.axis_index("spec")
    sea_list = sea_cells[0]
    flat = spectrum.reshape(comps, cells)
    wind_flat = wind.reshape(2, cells)
    mask = jnp.zeros((cells,), jnp.float32).at[sea_list].set(1.0)
    tile = cells // groups
    masked = flat * mask[None, :]
    points = lax.all_to_all(masked, "spec", split_axis=1, concat_axis=0, tiled=True)
    wind_tile = lax.dynamic_slice_in_dim(wind_flat, member * tile, tile, 1)
    updated = source_terms(points, wind_tile, transfer)
    energy = lax.all_to_all(updated, "spec", split_axis=0, concat_axis=1, tiled=True)
    field = energy.reshape(comps, rows, cols)
    cx = courant[0][:, None, None]
    cy = courant[1][:, None, None]
    mask_rows = mask.reshape(1, rows, cols)
    for step in range(SUB):
        padded = padded_2(field, (("space", 1),), 1)
        field = advance(padded, cx, cy) * mask_rows
    return field


def solution(mesh):
    in_specs = (
        P("spec", "space", None),
        P(None, "space", None),
        P(None, "spec"),
        P(),
        P("space", None),
    )
    out_specs = P("spec", "space", None)
    return jax.shard_map(body, mesh=mesh, in_specs=in_specs, out_specs=out_specs, check_vma=False)
```

profile of v0, /device:TPU:1, one launch (start us, length us, event | category | flops | bytes accessed | tf_op | source)
XLA Modules:
  0.0 329.2 jit_solution(8042034378633222551)
XLA Ops:
  0.7 10.0 %scatter_custom_fusion = f32[4096]{0:T(1024)S(1)} fusion(s32[1920]{0:T(1024)S(1)} %fusion.54, f32[1920]{0:T(1024)S(1)} %broadcast.86, f32[]{:T(128)} %constant.12.clone.1), kind=kCustom, calls=%fused_computation.76 | custom fusion | bytes 16388 | tf_op jit(solution)/shard_map/scatter | solution.py:75
  10.7 8.0 %copy_multiply_fusion = f32[324,4,1024]{2,0,1:T(8,128)} fusion(f32[324,4,1024]{2,1,0:T(4,128)} %param.5, f32[4,1024]{1,0:T(4,128)S(1)} %mul.243), kind=kLoop, calls=%fused_computation.65 | loop fusion | flops 1327104 | bytes 10633216 | tf_op jit(solution)/shard_map/mul | solution.py:77
  18.7 5.7 %all-to-all-start = ((f32[324,4,1024]{2,0,1:T(8,128)}), f32[324,4,1024]{2,0,1:T(8,128)}, u32[]{:S(2)}, u32[]{:S(2)}) async-start(f32[324,4,1024]{2,0,1:T(8,128)} %copy_multiply_fusion), calls=%async_computation | async-start | bytes 10747904 | tf_op jit(solution)/shard_map/all_to_all | solution.py:78
  25.2 59.6 %all-to-all-done = f32[324,4,1024]{2,0,1:T(8,128)} async-done(((f32[324,4,1024]{2,0,1:T(8,128)}), f32[324,4,1024]{2,0,1:T(8,128)}, u32[]{:S(2)}, u32[]{:S(2)}) %all-to-all-start) | async-done | bytes 5308448 | tf_op jit(solution)/shard_map/all_to_all | solution.py:78
  84.8 2.9 reduce_sum.36
  87.7 4.4 %all_to_all.26 = f32[1296,1024]{1,0:T(8,128)} reshape(f32[4,324,1024]{2,1,0:T(8,128)} %bitcast.1) | data formatting | bytes 10616832 | tf_op jit(solution)/shard_map/all_to_all | solution.py:78
  92.1 10.4 %fusion.69 = (f32[1024]{0:T(1024)S(1)}, f32[1296,1024]{1,0:T(8,128)S(1)}) fusion(bf16[1296,1296]{1,0:T(8,128)(2,1)} %param.8, f32[1296,1024]{1,0:T(8,128)} %all_to_all.26, f32[1024]{0:T(1024)S(1)} %broadcast_multiply_fusion.3, f32[1024]{0:T(1024)S(1)} %bitcast.31, f32[1296]{0:T(1024)S(1)} %mul.256, f32[1024]{0:T(1024)S(1)} %bitcast.27, ...), kind=kOutput, calls=%fused_computation.104 | convolution fusion | flops 3454450688 | bytes 14008000 | tf_op jit(solution)/shard_map/dot_general | solution.py:46
  102.4 5.6 %fusion.70 = (f32[1024]{0:T(1024)S(1)}, f32[1296,1024]{1,0:T(8,128)S(1)}) fusion(bf16[1296,1296]{1,0:T(8,128)(2,1)S(1)} %copy-done.3, f32[1296,1024]{1,0:T(8,128)S(1)} %get-tuple-element.36, f32[1024]{0:T(1024)S(1)} %broadcast_multiply_fusion.2, f32[1024]{0:T(1024)S(1)} %bitcast.32, f32[1296]{0:T(1024)S(1)} %mul.256, f32[1024]{0:T(1024)S(1)} %bitcast.28, ...), kind=kOutput, calls=%fused_computation.105 | convolution fusion | flops 3454450688 | bytes 14008000 | tf_op jit(solution)/shard_map/dot_general | solution.py:46
  108.0 5.6 %fusion.71 = (f32[1024]{0:T(1024)S(1)}, f32[1296,1024]{1,0:T(8,128)S(1)}) fusion(bf16[1296,1296]{1,0:T(8,128)(2,1)S(1)} %copy-done.3, f32[1296,1024]{1,0:T(8,128)S(1)} %get-tuple-element.38, f32[1024]{0:T(1024)S(1)} %broadcast_multiply_fusion.1, f32[1024]{0:T(1024)S(1)} %bitcast.33, f32[1296]{0:T(1024)S(1)} %mul.256, f32[1024]{0:T(1024)S(1)} %bitcast.29, ...), kind=kOutput, calls=%fused_computation.106 | convolution fusion | flops 3454450688 | bytes 14008000 | tf_op jit(solution)/shard_map/dot_general | solution.py:46
  113.6 7.0 %fusion.47 = f32[1296,1024]{1,0:T(8,128)} fusion(f32[1296,1024]{1,0:T(8,128)S(1)} %get-tuple-element.40, bf16[1296,1296]{1,0:T(8,128)(2,1)S(1)} %copy-done.3, f32[1024]{0:T(1024)S(1)} %broadcast_multiply_fusion, f32[1024]{0:T(1024)S(1)} %bitcast.34, f32[1296]{0:T(1024)S(1)} %mul.256, f32[1024]{0:T(1024)S(1)} %bitcast.30, f32[1296]{0:T(1024)S(1)} %mul.250, ...), kind=kOutput, calls=%fused_computation.69 | convolution fusion | flops 3453124608 | bytes 14003904 | tf_op jit(solution)/shard_map/dot_general | solution.py:46
  120.6 4.3 %all_to_all.27 = f32[4,324,1024]{2,1,0:T(8,128)} reshape(f32[1296,1024]{1,0:T(8,128)} %fusion.47) | data formatting | bytes 10616832 | tf_op jit(solution)/shard_map/all_to_all | solution.py:81
  124.9 62.8 %all_to_all.32 = f32[4,324,1024]{2,1,0:T(8,128)S(1)} all-to-all(f32[4,324,1024]{2,1,0:T(8,128)} %all_to_all.27), channel_id=1, replica_groups=mesh['spec'=4,'space'=8] {'spec'}, dimensions={0} | all-to-all | bytes 10616832 | tf_op jit(solution)/shard_map/all_to_all | solution.py:81
  189.4 4.4 %collective-permute-start.1 = (f32[324,1,1024]{2,1,0:T(1,128)S(1)}, f32[324,1,1024]{2,1,0:T(1,128)S(1)}, u32[]{:S(2)}, u32[]{:S(2)}) collective-permute-start(f32[324,1,1024]{2,1,0:T(1,128)S(1)} %copy.13), channel_id=1, source_target_pairs={{1,0},{2,1},{3,2},{4,3},{5,4},{6,5},{7,6},{9,8},{10,9},{11,10},{12... | collective-permute-start | bytes 3981320 | tf_op jit(solution)/shard_map/ppermute | solution.py:28
  195.1 3.2 collective-permute-start
  198.6 6.3 %fusion.66 = (f32[324,4,1023]{2,0,1:T(8,128)}, f32[324,4,1023]{2,0,1:T(8,128)}) fusion(f32[324,4,1024]{2,0,1:T(8,128)S(1)} %bitcast.23), kind=kLoop, calls=%fused_computation.101 | loop fusion | bytes 21212928 | tf_op jit(solution)/shard_map/jit(_roll_static)/slice | solution.py:57
  204.8 5.6 %collective-permute-done.1 = f32[324,1,1024]{2,1,0:T(1,128)S(1)} collective-permute-done((f32[324,1,1024]{2,1,0:T(1,128)S(1)}, f32[324,1,1024]{2,1,0:T(1,128)S(1)}, u32[]{:S(2)}, u32[]{:S(2)}) %collective-permute-start.1) | collective-permute-done | bytes 1327136 | tf_op jit(solution)/shard_map/ppermute | solution.py:28
  213.3 7.1 %fusion.32 = f32[324,4,1024]{2,0,1:T(8,128)S(1)} fusion(f32[324,4,1024]{2,0,1:T(8,128)S(1)} %bitcast.24, f32[324,1,1024]{2,0,1:T(8,128)S(1)} %copy.14, f32[324,1,1024]{2,0,1:T(8,128)S(1)} %copy.12, f32[324,4,1023]{2,0,1:T(8,128)} %get-tuple-element.28, f32[324,4,1]{2,0,1:T(8,128)S(1)} %get-tuple-element.30, f32[324,4,1]{2,0,1:T(8,128)S(1)} %get-tuple-element.29, ...), kind=kLoop, calls=%fused_computation.44 | loop fusion | flops 22560768 | bytes 23909440 | tf_op jit(solution)/shard_map/mul | solution.py:88
  225.4 4.4 %collective-permute-start.2 = (f32[324,1,1024]{2,1,0:T(1,128)S(1)}, f32[324,1,1024]{2,1,0:T(1,128)S(1)}, u32[]{:S(2)}, u32[]{:S(2)}) collective-permute-start(f32[324,1,1024]{2,1,0:T(1,128)S(1)} %copy.15), channel_id=1, source_target_pairs={{0,1},{1,2},{2,3},{3,4},{4,5},{5,6},{6,7},{8,9},{9,10},{10,11},{11... | collective-permute-start | bytes 3981320 | tf_op jit(solution)/shard_map/ppermute | solution.py:26
  230.1 6.3 %fusion.63 = (f32[324,4,1023]{2,0,1:T(8,128)}, f32[324,4,1023]{2,0,1:T(8,128)}) fusion(f32[324,4,1024]{2,0,1:T(8,128)S(1)} %fusion.32), kind=kLoop, calls=%fused_computation.98 | loop fusion | bytes 21212928 | tf_op jit(solution)/shard_map/jit(_roll_static)/slice | solution.py:57
  236.4 5.4 %collective-permute-done.3 = f32[324,1,1024]{2,1,0:T(1,128)S(1)} collective-permute-done((f32[324,1,1024]{2,1,0:T(1,128)S(1)}, f32[324,1,1024]{2,1,0:T(1,128)S(1)}, u32[]{:S(2)}, u32[]{:S(2)}) %collective-permute-start.3) | collective-permute-done | bytes 1327136 | tf_op jit(solution)/shard_map/ppermute | solution.py:28
  244.8 7.1 %fusion.23 = f32[324,4,1024]{2,0,1:T(8,128)S(1)} fusion(f32[324,4,1024]{2,0,1:T(8,128)S(1)} %fusion.32, f32[324,1,1024]{2,0,1:T(8,128)S(1)} %copy.18, f32[324,1,1024]{2,0,1:T(8,128)S(1)} %copy.16, f32[324,4,1023]{2,0,1:T(8,128)} %get-tuple-element.22, f32[324,4,1]{2,0,1:T(8,128)S(1)} %get-tuple-element.24, f32[324,4,1]{2,0,1:T(8,128)S(1)} %get-tuple-element.23, ...), kind=kLoop, calls=%fused_computation.33 | loop fusion | flops 22560768 | bytes 23909440 | tf_op jit(solution)/shard_map/mul | solution.py:88
  252.1 2.6 copy.21
  256.7 2.5 copy.19
  259.2 4.8 %collective-permute-start.4 = (f32[324,1,1024]{2,1,0:T(1,128)}, f32[324,1,1024]{2,1,0:T(1,128)}, u32[]{:S(2)}, u32[]{:S(2)}) collective-permute-start(f32[324,1,1024]{2,1,0:T(1,128)} %copy.19), channel_id=1, source_target_pairs={{0,1},{1,2},{2,3},{3,4},{4,5},{5,6},{6,7},{8,9},{9,10},{10,11},{11... | collective-permute-start | bytes 3981320 | tf_op jit(solution)/shard_map/ppermute | solution.py:26
  264.2 4.6 %fusion.60 = (f32[324,4,1023]{2,0,1:T(8,128)S(1)}, f32[324,4,1023]{2,0,1:T(8,128)}) fusion(f32[324,4,1024]{2,0,1:T(8,128)S(1)} %fusion.23), kind=kLoop, calls=%fused_computation.95 | loop fusion | bytes 21212928 | tf_op jit(solution)/shard_map/jit(_roll_static)/slice | solution.py:57
  268.8 6.0 %collective-permute-done.5 = f32[324,1,1024]{2,1,0:T(1,128)} collective-permute-done((f32[324,1,1024]{2,1,0:T(1,128)}, f32[324,1,1024]{2,1,0:T(1,128)}, u32[]{:S(2)}, u32[]{:S(2)}) %collective-permute-start.5) | collective-permute-done | bytes 1327136 | tf_op jit(solution)/shard_map/ppermute | solution.py:28
  280.2 8.9 %fusion.14 = f32[324,4,1024]{2,0,1:T(8,128)S(1)} fusion(f32[324,4,1024]{2,0,1:T(8,128)} %copy-done, f32[324,1,1024]{2,0,1:T(8,128)S(1)} %copy.22, f32[324,1,1024]{2,0,1:T(8,128)S(1)} %copy.20, f32[324,4,1023]{2,0,1:T(8,128)} %get-tuple-element.16, f32[324,4,1]{2,0,1:T(8,128)S(1)} %get-tuple-element.18, f32[324,4,1]{2,0,1:T(8,128)S(1)} %get-tuple-element.17, ...), kind=kLoop, calls=%fused_computation.22 | loop fusion | flops 22560768 | bytes 23909440 | tf_op jit(solution)/shard_map/mul | solution.py:88
  296.1 4.5 %collective-permute-start.6 = (f32[324,1,1024]{2,1,0:T(1,128)}, f32[324,1,1024]{2,1,0:T(1,128)}, u32[]{:S(2)}, u32[]{:S(2)}) collective-permute-start(f32[324,1,1024]{2,1,0:T(1,128)} %copy.23), channel_id=1, source_target_pairs={{0,1},{1,2},{2,3},{3,4},{4,5},{5,6},{6,7},{8,9},{9,10},{10,11},{11... | collective-permute-start | bytes 3981320 | tf_op jit(solution)/shard_map/ppermute | solution.py:26
  300.9 4.6 %fusion.57 = (f32[324,4,1023]{2,0,1:T(8,128)S(1)}, f32[324,4,1023]{2,0,1:T(8,128)}) fusion(f32[324,4,1024]{2,0,1:T(8,128)S(1)} %fusion.14), kind=kLoop, calls=%fused_computation.92 | loop fusion | bytes 21212928 | tf_op jit(solution)/shard_map/jit(_roll_static)/slice | solution.py:57
  305.5 6.4 %collective-permute-done.7 = f32[324,1,1024]{2,1,0:T(1,128)} collective-permute-done((f32[324,1,1024]{2,1,0:T(1,128)}, f32[324,1,1024]{2,1,0:T(1,128)}, u32[]{:S(2)}, u32[]{:S(2)}) %collective-permute-start.7) | collective-permute-done | bytes 1327136 | tf_op jit(solution)/shard_map/ppermute | solution.py:28
  317.1 6.1 %fusion.5 = f32[324,4,1024]{2,0,1:T(8,128)S(1)} fusion(f32[324,4,1024]{2,0,1:T(8,128)S(1)} %fusion.14, f32[324,1,1024]{2,0,1:T(8,128)S(1)} %copy.26, f32[324,1,1024]{2,0,1:T(8,128)S(1)} %copy.24, f32[324,4,1023]{2,0,1:T(8,128)} %get-tuple-element.10, f32[324,4,1]{2,0,1:T(8,128)S(1)} %get-tuple-element.12, f32[324,4,1]{2,0,1:T(8,128)S(1)} %get-tuple-element.11, ...), kind=kLoop, calls=%fused_computation.11 | loop fusion | flops 22560768 | bytes 23909440 | tf_op jit(solution)/shard_map/mul | solution.py:88
  323.2 5.8 %copy.27 = f32[324,4,1024]{2,1,0:T(4,128)} copy(f32[324,4,1024]{2,0,1:T(8,128)S(1)} %fusion.5) | data formatting | bytes 10616832 | tf_op jit(solution)/shard_map/mul | solution.py:88
  (56 shorter events, 35.8 us)
Async XLA Ops:
  18.7 6.3 %copy-start.1 = (f32[2,4,1024]{2,1,0:T(4,128)S(1)}, f32[2,4,1024]{2,1,0:T(4,128)}, u32[]{:S(2)}) copy-start(f32[2,4,1024]{2,1,0:T(4,128)} %param.6) | copy-start | bytes 98308
  18.7 66.1 %all-to-all-start = ((f32[324,4,1024]{2,0,1:T(8,128)}), f32[324,4,1024]{2,0,1:T(8,128)}, u32[]{:S(2)}, u32[]{:S(2)}) async-start(f32[324,4,1024]{2,0,1:T(8,128)} %copy_multiply_fusion), calls=%async_computation | async-start | bytes 10747904 | tf_op jit(solution)/shard_map/all_to_all | solution.py:78
  92.1 10.4 %copy-start.3 = (bf16[1296,1296]{1,0:T(8,128)(2,1)S(1)}, bf16[1296,1296]{1,0:T(8,128)(2,1)}, u32[]{:S(2)}) copy-start(bf16[1296,1296]{1,0:T(8,128)(2,1)} %param.8) | copy-start | bytes 10077700
  187.8 10.5 %copy-start.2 = (f32[2,324]{1,0:T(2,128)S(1)}, f32[2,324]{1,0:T(2,128)}, u32[]{:S(2)}) copy-start(f32[2,324]{1,0:T(2,128)} %param.7) | copy-start | bytes 7780
  189.4 21.1 %collective-permute-start.1 = (f32[324,1,1024]{2,1,0:T(1,128)S(1)}, f32[324,1,1024]{2,1,0:T(1,128)S(1)}, u32[]{:S(2)}, u32[]{:S(2)}) collective-permute-start(f32[324,1,1024]{2,1,0:T(1,128)S(1)} %copy.13), channel_id=1, source_target_pairs={{1,0},{2,1},{3,2},{4,3},{5,4},{6,5},{7,6},{9,8},{10,9},{11,10},{12... | collective-permute-start | bytes 3981320 | tf_op jit(solution)/shard_map/ppermute | solution.py:28
  195.1 17.9 %collective-permute-start = (f32[324,1,1024]{2,1,0:T(1,128)S(1)}, f32[324,1,1024]{2,1,0:T(1,128)S(1)}, u32[]{:S(2)}, u32[]{:S(2)}) collective-permute-start(f32[324,1,1024]{2,1,0:T(1,128)S(1)} %copy.11), channel_id=1, source_target_pairs={{0,1},{1,2},{2,3},{3,4},{4,5},{5,6},{6,7},{8,9},{9,10},{10,11},{11... | collective-permute-start | bytes 3981320 | tf_op jit(solution)/shard_map/ppermute | solution.py:26
  221.9 19.8 %collective-permute-start.3 = (f32[324,1,1024]{2,1,0:T(1,128)S(1)}, f32[324,1,1024]{2,1,0:T(1,128)S(1)}, u32[]{:S(2)}, u32[]{:S(2)}) collective-permute-start(f32[324,1,1024]{2,1,0:T(1,128)S(1)} %copy.17), channel_id=1, source_target_pairs={{1,0},{2,1},{3,2},{4,3},{5,4},{6,5},{7,6},{9,8},{10,9},{11,10},{12... | collective-permute-start | bytes 3981320 | tf_op jit(solution)/shard_map/ppermute | solution.py:28
  225.4 19.1 %collective-permute-start.2 = (f32[324,1,1024]{2,1,0:T(1,128)S(1)}, f32[324,1,1024]{2,1,0:T(1,128)S(1)}, u32[]{:S(2)}, u32[]{:S(2)}) collective-permute-start(f32[324,1,1024]{2,1,0:T(1,128)S(1)} %copy.15), channel_id=1, source_target_pairs={{0,1},{1,2},{2,3},{3,4},{4,5},{5,6},{6,7},{8,9},{9,10},{10,11},{11... | collective-permute-start | bytes 3981320 | tf_op jit(solution)/shard_map/ppermute | solution.py:26
  251.9 12.3 %copy-start = (f32[324,4,1024]{2,0,1:T(8,128)}, f32[324,4,1024]{2,0,1:T(8,128)S(1)}, u32[]{:S(2)}) copy-start(f32[324,4,1024]{2,0,1:T(8,128)S(1)} %fusion.23) | copy-start | bytes 15925252
  254.7 20.2 %collective-permute-start.5 = (f32[324,1,1024]{2,1,0:T(1,128)}, f32[324,1,1024]{2,1,0:T(1,128)}, u32[]{:S(2)}, u32[]{:S(2)}) collective-permute-start(f32[324,1,1024]{2,1,0:T(1,128)} %copy.21), channel_id=1, source_target_pairs={{1,0},{2,1},{3,2},{4,3},{5,4},{6,5},{7,6},{9,8},{10,9},{11,10},{12... | collective-permute-start | bytes 3981320 | tf_op jit(solution)/shard_map/ppermute | solution.py:28
  259.2 19.4 %collective-permute-start.4 = (f32[324,1,1024]{2,1,0:T(1,128)}, f32[324,1,1024]{2,1,0:T(1,128)}, u32[]{:S(2)}, u32[]{:S(2)}) collective-permute-start(f32[324,1,1024]{2,1,0:T(1,128)} %copy.19), channel_id=1, source_target_pairs={{0,1},{1,2},{2,3},{3,4},{4,5},{5,6},{6,7},{8,9},{9,10},{10,11},{11... | collective-permute-start | bytes 3981320 | tf_op jit(solution)/shard_map/ppermute | solution.py:26
  291.7 20.2 %collective-permute-start.7 = (f32[324,1,1024]{2,1,0:T(1,128)}, f32[324,1,1024]{2,1,0:T(1,128)}, u32[]{:S(2)}, u32[]{:S(2)}) collective-permute-start(f32[324,1,1024]{2,1,0:T(1,128)} %copy.25), channel_id=1, source_target_pairs={{1,0},{2,1},{3,2},{4,3},{5,4},{6,5},{7,6},{9,8},{10,9},{11,10},{12... | collective-permute-start | bytes 3981320 | tf_op jit(solution)/shard_map/ppermute | solution.py:28
  296.1 19.4 %collective-permute-start.6 = (f32[324,1,1024]{2,1,0:T(1,128)}, f32[324,1,1024]{2,1,0:T(1,128)}, u32[]{:S(2)}, u32[]{:S(2)}) collective-permute-start(f32[324,1,1024]{2,1,0:T(1,128)} %copy.23), channel_id=1, source_target_pairs={{0,1},{1,2},{2,3},{3,4},{4,5},{5,6},{6,7},{8,9},{9,10},{10,11},{11... | collective-permute-start | bytes 3981320 | tf_op jit(solution)/shard_map/ppermute | solution.py:26
where the time goes:
time: 334 us; the launch traced here: 329 us
  waiting for transfers between devices  91.9 us (28%)
  local copies, waits for them, and re-layouts  71.5 us (21%)
  blocking collectives  62.8 us (19%)
  other arithmetic  41 us (12%)
  starting transfers between devices  32.9 us (10%)
  matrix products  28.5 us (9%)
    all_to_all x1, blocking collectives, body(): lax.all_to_all(updated, 'spec', split_axis=0, concat_axis=1, tiled=True)  62.8 us
    all_to_all x1, waiting for transfers between devices, body(): lax.all_to_all(masked, 'spec', split_axis=1, concat_axis=0, tiled=True)  59.6 us
    mul x4, other arithmetic, body(): field = advance(padded, cx, cy) * mask_rows  29.2 us
    dot_general x4, matrix products, source_terms(): moved = jnp.dot(transfer, low, preferred_element_type=jnp.float32)  28.5 us
    ppermute x4, waiting for transfers between devices, padded_2(): lax.ppermute(head, axis, [((i + 1) % count, i) for i in range(ends)])  23.5 us
    slice x8, local copies, waits for them, and re-layouts, advance(): right = jnp.roll(centre, -1, axis=2)  22.8 us
    ppermute x4, starting transfers between devices, padded_2(): lax.ppermute(tail, axis, [(i, (i + 1) % count) for i in range(ends)])  16.9 us
    ppermute x4, starting transfers between devices, padded_2(): lax.ppermute(head, axis, [((i + 1) % count, i) for i in range(ends)])  10.3 us
  transfers between devices with their start and end apart: 9, of which 9 were waited for; matrix products, arithmetic and copies ran while one was open for 11% of the time, Pallas kernels for 0%

commit v1 on v0

--- a/solution.py
+++ b/solution.py
@@ -2,7 +2,10 @@
 
 import jax
 import jax.numpy as jnp
+import numpy as np
 from jax import lax
+from jax.experimental import pallas as pl
+from jax.experimental.pallas import tpu as pltpu
 from jax.sharding import PartitionSpec as P
 
 NDIR = 36
@@ -89,7 +92,327 @@
     return field
 
 
+LANES = 128
+MESH = pl.DeviceIdType.MESH
+
+
+def fits(mesh, spectrum, wind, courant, transfer, sea_cells):
+    groups = mesh.shape["spec"]
+    cells = spectrum.shape[1] * spectrum.shape[2]
+    tile = cells // groups
+    return (
+        groups == 4
+        and tile % (8 * LANES) == 0
+        and spectrum.shape[2] % LANES == 0
+        and sea_cells.shape[1] == 15 * LANES
+        and spectrum.shape[1] == SUB
+    )
+
+
+def compact_kernel(sea, spectrum, wind, blocks, winds, sem, wind_sem):
+    per_row = spectrum.shape[2] // LANES
+    count = blocks.shape[0]
+    copies = []
+    for q in range(count - 1):
+        place = lax.div(sea[0, q * LANES], LANES)
+        row = lax.div(place, per_row)
+        col = pl.multiple_of(lax.rem(place, per_row) * LANES, LANES)
+        copies.append(pltpu.make_async_copy(spectrum.at[:, row, pl.ds(col, LANES)], blocks.at[q], sem.at[q]))
+        copies.append(pltpu.make_async_copy(wind.at[:, row, pl.ds(col, LANES)], winds.at[q], wind_sem.at[q]))
+    for copy in copies:
+        copy.start()
+    blocks[count - 1] = jnp.zeros(blocks.shape[1:], blocks.dtype)
+    winds[count - 1] = jnp.zeros(winds.shape[1:], winds.dtype)
+    for copy in copies:
+        copy.wait()
+
+
+def relatives(s):
+    return (s + 1 - 2 * lax.rem(s, 2), lax.rem(s + 2, 4), 3 - s)
+
+
+def exchange_kernel(ends, blocks, winds, trig, transfer, out, came, points, low, gamma, made,
+                    in_send, in_recv, out_send, out_recv, halo_send, halo_recv, own_sem, kept_sem):
+    s = lax.axis_index("spec")
+    z = lax.axis_index("space")
+    peers = relatives(s)
+    comps = blocks.shape[1]
+    count = blocks.shape[0]
+    chunks = count // 4
+    total = points.shape[0]
+
+    barrier = pltpu.get_barrier_semaphore()
+    for peer in peers:
+        pl.semaphore_signal(barrier, inc=1, device_id={"spec": peer}, device_id_type=MESH)
+
+    @pl.when(z > 0)
+    def _():
+        pl.semaphore_signal(barrier, inc=1, device_id={"space": z - 1}, device_id_type=MESH)
+
+    @pl.when(z < ends)
+    def _():
+        pl.semaphore_signal(barrier, inc=1, device_id={"space": z + 1}, device_id_type=MESH)
+
+    pl.semaphore_wait(barrier, 3 + jnp.minimum(z, 1) + jnp.minimum(ends - z, 1))
+
+    def inward(c, j, sending):
+        source = blocks.at[chunks * peers[j] + c]
+        target = came.at[c, s if sending else peers[j]]
+        return pltpu.make_async_remote_copy(
+            src_ref=source, dst_ref=target, send_sem=in_send.at[c, j], recv_sem=in_recv.at[c, j],
+            device_id={"spec": peers[j]}, device_id_type=MESH)
+
+    def outward(c, j, sending):
+        source = made.at[c, peers[j]]
+        target = out.at[count + chunks * (s if sending else peers[j]) + c]
+        return pltpu.make_async_remote_copy(
+            src_ref=source, dst_ref=target, send_sem=out_send.at[c, j], recv_sem=out_recv.at[c, j],
+            device_id={"spec": peers[j]}, device_id_type=MESH)
+
+    def own(c):
+        return pltpu.make_async_copy(blocks.at[chunks * s + c], came.at[c, s], own_sem.at[c])
+
+    def kept(c):
+        return pltpu.make_async_copy(made.at[c, s], out.at[count + chunks * s + c], kept_sem.at[c])
+
+    def halo(q, way):
+        return pltpu.make_async_remote_copy(
+            src_ref=out.at[count + q], dst_ref=out.at[q + 2 * way * count],
+            send_sem=halo_send.at[way, q], recv_sem=halo_recv.at[way, q],
+            device_id={"space": z + 1 - 2 * way}, device_id_type=MESH)
+
+    for c in range(chunks):
+        own(c).start()
+        for j in (2, 0, 1):
+            inward(c, j, True).start()
+
+    def chunk(c, carry):
+        own(c).wait()
+        for j in range(3):
+            inward(c, j, False).wait_recv()
+        for p in range(4):
+            points[p * comps:(p + 1) * comps, :] = came[c, p]
+        pair = winds[chunks * s + c]
+        drive = jnp.maximum(trig[:, 0:1] * pair[0:1, :] + trig[:, 1:2] * pair[1:2, :], 0.0)
+        gamma[...] = trig[:, 2:3] * drive
+
+        def source(step, carry):
+            e = points[...]
+            low[...] = e.astype(jnp.bfloat16)
+            mean = jnp.sum(e, axis=0, keepdims=True) * (1.0 / total)
+            moved = jnp.dot(transfer[...], low[...], preferred_element_type=jnp.float32)
+            points[...] = e + (gamma[...] - whitecap * mean) * e + moved
+            return carry
+
+        lax.fori_loop(0, SRC_STEPS, source, 0)
+        for p in range(4):
+            made[c, p] = points[p * comps:(p + 1) * comps, :]
+        for j in (2, 0, 1):
+            outward(c, j, True).start()
+        kept(c).start()
+        return carry
+
+    lax.fori_loop(0, chunks, chunk, 0)
+
+    def send_halo(q):
+        @pl.when(z < ends)
+        def _():
+            halo(q, 0).start()
+
+        @pl.when(z > 0)
+        def _():
+            halo(q, 1).start()
+
+    def spread(c, carry):
+        kept(c).wait()
+        send_halo(chunks * s + c)
+        for j in range(3):
+            outward(c, j, False).wait_recv()
+            send_halo(chunks * peers[j] + c)
+        return carry
+
+    lax.fori_loop(0, chunks, spread, 0)
+
+    def finish(c, carry):
+        for j in range(3):
+            inward(c, j, True).wait_send()
+            outward(c, j, True).wait_send()
+        return carry
+
+    lax.fori_loop(0, chunks, finish, 0)
+
+    def finish_halo(q, carry):
+        @pl.when(z < ends)
+        def _():
+            halo(q, 0).wait_send()
+            halo(q, 1).wait_recv()
+
+        @pl.when(z > 0)
+        def _():
+            halo(q, 1).wait_send()
+            halo(q, 0).wait_recv()
+
+        return carry
+
+    lax.fori_loop(0, count, finish_halo, 0)
+
+
+def advance_kernel(ends, sea, blocks, coef, out, first, second, bank, table, places, sems, zero_sem):
+    z = lax.axis_index("space")
+    comps = coef.shape[0]
+    count = blocks.shape[0] // 3
+    rows, per_row = out.shape[1], out.shape[2] // LANES
+    span = rows * per_row
+    empty = 2 * count - 1
+    live = count - 1
+
+    def clear(i, carry):
+        table[i] = empty
+        return carry
+
+    lax.fori_loop(0, (3 * rows + 2) * per_row, clear, 0)
+    for slab in range(3):
+        present = jnp.logical_and(z + slab - 1 >= 0, z + slab - 1 <= ends)
+
+        def note(q, carry):
+            place = lax.div(sea[slab, q * LANES], LANES) + slab * span
+            places[slab * live + q] = place
+
+            @pl.when(present)
+            def _():
+                table[per_row + place] = slab * count + q
+
+            return carry
+
+        lax.fori_loop(0, live, note, 0)
+
+    cx = coef[:, 0:1]
+    cy = coef[:, 1:2]
+    wide = (comps, LANES)
+    bank[0] = jnp.broadcast_to(1.0 - jnp.abs(cx) - jnp.abs(cy), wide)
+    bank[1] = jnp.broadcast_to(jnp.maximum(cx, 0.0), wide)
+    bank[2] = jnp.broadcast_to(-jnp.minimum(cx, 0.0), wide)
+    bank[3] = jnp.broadcast_to(cy, wide)
+    first[empty] = jnp.zeros(wide, jnp.float32)
+    second[empty] = jnp.zeros(wide, jnp.float32)
+    lane = lax.broadcasted_iota(jnp.int32, wide, 1)
+
+    def write(i):
+        row = lax.div(i, per_row)
+        col = pl.multiple_of(lax.rem(i, per_row) * LANES, LANES)
+        return row, col
+
+    for step in range(SUB):
+        old = blocks if step == 0 else (first, second)[(step + 1) % 2]
+        new = (first, second)[step % 2]
+
+        def one(n, carry):
+            place = places[n]
+            row = lax.div(place, per_row)
+            col = lax.rem(place, per_row)
+            mine = table[per_row + place]
+            due = jnp.logical_and(jnp.logical_and(row >= 1 + step, row <= 3 * rows - 2 - step), mine != empty)
+
+            @pl.when(due)
+            def _():
+                start = per_row + row * per_row
+                left = table[start + lax.rem(col + per_row - 1, per_row)]
+                right = table[start + lax.rem(col + 1, per_row)]
+                e = old[mine]
+                to_right = pltpu.roll(jnp.where(lane == LANES - 1, old[left], e), 1, 1)
+                to_left = pltpu.roll(jnp.where(lane == 0, old[right], e), LANES - 1, 1)
+                across = bank[3]
+                side = jnp.where(across > 0.0, to_right, to_left)
+                new[mine] = (bank[0] * e + bank[1] * old[table[place]] + bank[2] * old[table[place + 2 * per_row]]
+                             + jnp.abs(across) * side)
+
+            return carry
+
+        lax.fori_loop(0, 3 * live, one, 0)
+
+    final = (first, second)[(SUB - 1) % 2]
+
+    def put(i):
+        row, col = write(i)
+        return pltpu.make_async_copy(
+            final.at[table[per_row + span + i]], out.at[:, row, pl.ds(col, LANES)], sems.at[i])
+
+    lax.fori_loop(0, span, lambda i, c: (put(i).start(), c)[1], 0)
+    lax.fori_loop(0, span, lambda i, c: (put(i).wait(), c)[1], 0)
+
+
+def fast_body(spectrum, wind, courant, transfer, sea_cells):
+    comps, rows, cols = spectrum.shape
+    total = transfer.shape[0]
+    count = sea_cells.shape[1] // LANES + 1
+    chunks = count // 4
+    ends = lax.axis_size("space") - 1
+    dma = pltpu.SemaphoreType.DMA
+    vmem = pl.BlockSpec(memory_space=pltpu.VMEM)
+    smem = pl.BlockSpec(memory_space=pltpu.SMEM)
+    hbm = pl.BlockSpec(memory_space=pl.ANY)
+    f32 = jnp.float32
+
+    above = lax.ppermute(sea_cells, "space", [(i, i + 1) for i in range(ends)])
+    below = lax.ppermute(sea_cells, "space", [(i + 1, i) for i in range(ends)])
+    seas = jnp.concatenate([above, sea_cells, below], axis=0)
+
+    blocks, winds = pl.pallas_call(
+        compact_kernel,
+        out_shape=(jax.ShapeDtypeStruct((count, comps, LANES), f32), jax.ShapeDtypeStruct((count, 2, LANES), f32)),
+        in_specs=[smem, hbm, hbm],
+        out_specs=(vmem, vmem),
+        scratch_shapes=[dma((count,)), dma((count,))],
+        name="compact",
+    )(sea_cells, spectrum, wind)
+
+    angle = np.arange(NDIR, dtype=np.float32) * np.float32(2.0 * math.pi / NDIR)
+    growth = np.float32(growth_rate) * (np.arange(NFREQ, dtype=np.float32) + 1.0) / NFREQ
+    trig = jnp.asarray(np.stack([
+        np.repeat(np.cos(angle), NFREQ), np.repeat(np.sin(angle), NFREQ), np.tile(growth, NDIR)], axis=1), f32)
+
+    slabs = pl.pallas_call(
+        lambda *refs: exchange_kernel(ends, *refs),
+        out_shape=jax.ShapeDtypeStruct((3 * count, comps, LANES), f32),
+        in_specs=[vmem, vmem, vmem, vmem],
+        out_specs=hbm,
+        scratch_shapes=[
+            pltpu.VMEM((chunks, 4, comps, LANES), f32),
+            pltpu.VMEM((total, LANES), f32),
+            pltpu.VMEM((total, LANES), jnp.bfloat16),
+            pltpu.VMEM((total, LANES), f32),
+            pltpu.VMEM((chunks, 4, comps, LANES), f32),
+            dma((chunks, 3)), dma((chunks, 3)), dma((chunks, 3)), dma((chunks, 3)),
+            dma((2, count)), dma((2, count)), dma((chunks,)), dma((chunks,)),
+        ],
+        compiler_params=pltpu.CompilerParams(collective_id=0, has_side_effects=True, vmem_limit_bytes=48 << 20),
+        name="exchange",
+    )(blocks, winds, trig, transfer)
+
+    return pl.pallas_call(
+        lambda *refs: advance_kernel(ends, *refs),
+        out_shape=jax.ShapeDtypeStruct(spectrum.shape, f32),
+        in_specs=[smem, vmem, vmem],
+        out_specs=hbm,
+        scratch_shapes=[
+            pltpu.VMEM((3 * count, comps, LANES), f32),
+            pltpu.VMEM((3 * count, comps, LANES), f32),
+            pltpu.VMEM((4, comps, LANES), f32),
+            pltpu.SMEM(((3 * rows + 2) * (cols // LANES),), jnp.int32),
+            pltpu.SMEM((3 * count,), jnp.int32),
+            dma((rows * (cols // LANES),)), dma,
+        ],
+        compiler_params=pltpu.CompilerParams(vmem_limit_bytes=48 << 20),
+        name="advance",
+    )(seas, slabs, courant.T)
+
+
 def solution(mesh):
+    def step(*args):
+        if fits(mesh, *args):
+            return fast_body(*args)
+        return body(*args)
+
     in_specs = (
         P("spec", "space", None),
         P(None, "space", None),
@@ -98,4 +421,4 @@
         P("space", None),
     )
     out_specs = P("spec", "space", None)
-    return jax.shard_map(body, mesh=mesh, in_specs=in_specs, out_specs=out_specs, check_vma=False)
+    return jax.shard_map(step, mesh=mesh, in_specs=in_specs, out_specs=out_specs, check_vma=False)

time: 334 us -> 118 us (0.35); the launches traced: 329 us -> 118 us
  Pallas kernels: 0 us -> 108 us
  waiting for transfers between devices: 91.9 us -> 0.01 us
  local copies, waits for them, and re-layouts: 71.5 us -> 3.29 us
  blocking collectives: 62.8 us -> 0 us
  other arithmetic: 41 us -> 0.02 us
  matrix products: 28.5 us -> 0 us
  starting transfers between devices: 32.9 us -> 6.63 us
    pallas_call x0 -> x3, Pallas kernels: none -> 108 us  [the longest x1 72.4 us: fast_body(): pl.pallas_call(lambda *refs: exchange_kernel(ends, *refs), out_shape=jax....]
    all_to_all x1 -> x0, blocking collectives: 62.8 us -> none  [body(): lax.all_to_all(updated, 'spec', split_axis=0, concat_axis=1, tiled=True)]
    all_to_all x1 -> x0, waiting for transfers between devices: 59.6 us -> none  [body(): lax.all_to_all(masked, 'spec', split_axis=1, concat_axis=0, tiled=True)]
    slice x21 -> x0, local copies, waits for them, and re-layouts: 39 us -> none  [the longest x8 22.8 us: advance(): right = jnp.roll(centre, -1, axis=2)]
    mul x9 -> x0, other arithmetic: 37.2 us -> none  [the longest x4 29.2 us: body(): field = advance(padded, cx, cy) * mask_rows]
    ppermute x8 -> x2, waiting for transfers between devices: 32.3 us -> 0.01 us  [the longest x1 0.01 us: fast_body(): below = lax.ppermute(sea_cells, 'space', [(i + 1, i) for i in range(ends)])]
    dot_general x4 -> x0, matrix products: 28.5 us -> none  [source_terms(): moved = jnp.dot(transfer, low, preferred_element_type=jnp.float32)]
    ppermute x8 -> x2, starting transfers between devices: 27.2 us -> 6.63 us  [the longest x1 4.58 us: fast_body(): above = lax.ppermute(sea_cells, 'space', [(i, i + 1) for i in range(ends)])]
  transfers between devices with their start and end apart: 9 -> 2, of which waited for: 9 -> 0; matrix products, arithmetic and copies ran while one was open for 11% -> 1% of each run, Pallas kernels for 0% -> 66%
where the time goes in v1:
time: 118 us
  Pallas kernels  108 us (92%)
  starting transfers between devices  6.63 us (6%)
  local copies, waits for them, and re-layouts  3.29 us (3%)
    pallas_call x1, Pallas kernels, fast_body(): pl.pallas_call(lambda *refs: exchange_kernel(ends, *refs), out_shape=jax....  72.4 us
    pallas_call x1, Pallas kernels, fast_body(): pl.pallas_call(lambda *refs: advance_kernel(ends, *refs), out_shape=jax.S...  30.4 us
    pallas_call x1, Pallas kernels, fast_body(): pl.pallas_call(compact_kernel, out_shape=(jax.ShapeDtypeStruct((count, co...  4.7 us
    ppermute x1, starting transfers between devices, fast_body(): above = lax.ppermute(sea_cells, 'space', [(i, i + 1) for i in range(ends)])  4.58 us
    unnamed x9, local copies, waits for them, and re-layouts  3.29 us
  transfers between devices with their start and end apart: 2, of which 0 were waited for; matrix products, arithmetic and copies ran while one was open for 1% of the time, Pallas kernels for 66%

profile of v1, /device:TPU:1, one launch (start us, length us, event | category | flops | bytes accessed | tf_op | source)
XLA Modules:
  0.0 117.6 jit_solution(3291252218188767117)
XLA Ops:
  0.0 0.0 copy-start.1
  0.0 2.0 %collective-permute-start.1 = (s32[1,1920]{1,0:T(1,128)}, s32[1,1920]{1,0:T(1,128)S(1)}, u32[]{:S(2)}, u32[]{:S(2)}) collective-permute-start(s32[1,1920]{1,0:T(1,128)} %sea.1), channel_id=1, source_target_pairs={{1,0},{2,1},{3,2},{4,3},{5,4},{6,5},{7,6},{9,8},{10,9},{11,10},{12... | collective-permute-start | bytes 23048 | tf_op jit(solution)/shard_map/ppermute | solution.py:357
  2.1 4.6 %collective-permute-start = (s32[1,1920]{1,0:T(1,128)}, s32[1,1920]{1,0:T(1,128)S(1)}, u32[]{:S(2)}, u32[]{:S(2)}) collective-permute-start(s32[1,1920]{1,0:T(1,128)} %sea.1), channel_id=1, source_target_pairs={{0,1},{1,2},{2,3},{3,4},{4,5},{5,6},{6,7},{8,9},{9,10},{10,11},{11... | collective-permute-start | bytes 23048 | tf_op jit(solution)/shard_map/ppermute | solution.py:356
  6.6 0.8 copy.7
  7.5 4.7 %compact.1 = (f32[16,324,128]{2,1,0:T(8,128)}, f32[16,2,128]{2,1,0:T(2,128)}) custom-call(s32[1,1920]{1,0:T(1,128)} %sea.1, f32[324,4,1024]{2,1,0:T(4,128)} %spectrum.1, f32[2,4,1024]{2,1,0:T(4,128)} %wind.1), custom_call_target="tpu_custom_call" | custom-call | tf_op jit(solution)/shard_map/compact/pallas_call | solution.py:360
  12.2 0.0 copy-done.1
  12.2 0.0 copy-start
  12.2 1.7 %copy-done = f32[16,324,128]{2,1,0:T(8,128)S(1)} copy-done((f32[16,324,128]{2,1,0:T(8,128)S(1)}, f32[16,324,128]{2,1,0:T(8,128)}, u32[]{:S(2)}) %copy-start) | copy-done | bytes 2654232
  13.9 0.0 copy-start.2
  13.9 0.7 copy-done.2
  14.7 0.0 copy-start.3
  14.7 72.4 %exchange.1.refs_1_ = f32[48,324,128]{2,1,0:T(8,128)} custom-call(f32[16,324,128]{2,1,0:T(8,128)S(1)} %copy-done, f32[16,2,128]{2,1,0:T(2,128)S(1)} %copy-done.2, f32[1296,3]{1,0:T(8,128)S(1)} %copy-done.1, bf16[1296,1296]{1,0:T(8,128)(2,1)} %refs_3_.1), custom_call_target="tpu_custom_call" | custom-call | tf_op jit(solution)/shard_map/exchange/pallas_call | solution.py:374
  87.1 0.0 collective-permute-done.1
  87.1 0.0 collective-permute-done
  87.1 0.0 copy-done.3
  87.2 30.4 %advance.1 = f32[324,4,1024]{2,1,0:T(4,128)} custom-call(s32[3,1920]{1,0:T(4,128)S(1)} %pad_add_fusion.refs_0_, f32[48,324,128]{2,1,0:T(8,128)} %exchange.1.refs_1_, f32[324,2]{1,0:T(8,128)S(1)} %bitcast.1), custom_call_target="tpu_custom_call" | custom-call | tf_op jit(solution)/shard_map/advance/pallas_call | solution.py:392
  (1 shorter events, 0.0 us)
Async XLA Ops:
  0.0 12.2 %copy-start.1 = (f32[1296,3]{1,0:T(8,128)S(1)}, f32[1296,3]{1,0:T(8,128)}, u32[]{:S(2)}) copy-start(f32[1296,3]{1,0:T(8,128)} %constant.2.clone.refs_2_) | copy-start | bytes 46660
  0.0 87.1 %collective-permute-start.1 = (s32[1,1920]{1,0:T(1,128)}, s32[1,1920]{1,0:T(1,128)S(1)}, u32[]{:S(2)}, u32[]{:S(2)}) collective-permute-start(s32[1,1920]{1,0:T(1,128)} %sea.1), channel_id=1, source_target_pairs={{1,0},{2,1},{3,2},{4,3},{5,4},{6,5},{7,6},{9,8},{10,9},{11,10},{12... | collective-permute-start | bytes 23048 | tf_op jit(solution)/shard_map/ppermute | solution.py:357
  2.1 85.0 %collective-permute-start = (s32[1,1920]{1,0:T(1,128)}, s32[1,1920]{1,0:T(1,128)S(1)}, u32[]{:S(2)}, u32[]{:S(2)}) collective-permute-start(s32[1,1920]{1,0:T(1,128)} %sea.1), channel_id=1, source_target_pairs={{0,1},{1,2},{2,3},{3,4},{4,5},{5,6},{6,7},{8,9},{9,10},{10,11},{11... | collective-permute-start | bytes 23048 | tf_op jit(solution)/shard_map/ppermute | solution.py:356
  12.2 1.8 %copy-start = (f32[16,324,128]{2,1,0:T(8,128)S(1)}, f32[16,324,128]{2,1,0:T(8,128)}, u32[]{:S(2)}) copy-start(f32[16,324,128]{2,1,0:T(8,128)} %get-tuple-element.7.refs_0_) | copy-start | bytes 7962628
  13.9 0.7 copy-start.2
  14.7 72.5 %copy-start.3 = (s32[1,1920]{1,0:T(1,128)S(1)}, s32[1,1920]{1,0:T(1,128)}, u32[]{:S(2)}) copy-start(s32[1,1920]{1,0:T(1,128)} %sea.1) | copy-start | bytes 23044

commit v2 on v0

--- a/solution.py
+++ b/solution.py
@@ -2,7 +2,10 @@
 
 import jax
 import jax.numpy as jnp
+import numpy as np
 from jax import lax
+from jax.experimental import pallas as pl
+from jax.experimental.pallas import tpu as pltpu
 from jax.sharding import PartitionSpec as P
 
 NDIR = 36
@@ -89,7 +92,424 @@
     return field
 
 
+LANES = 128
+NO_ROW = -5000
+NO_COLUMN = -1000
+GROUP = 56
+MESH = pl.DeviceIdType.MESH
+
+
+def fits(mesh, spectrum, wind, courant, transfer, sea_cells):
+    groups = mesh.shape["spec"]
+    cells = spectrum.shape[1] * spectrum.shape[2]
+    tile = cells // groups
+    return (
+        groups == 4
+        and tile % (8 * LANES) == 0
+        and spectrum.shape[2] % LANES == 0
+        and sea_cells.shape[1] == 15 * LANES
+        and spectrum.shape[1] == SUB
+    )
+
+
+def compact_kernel(sea, spectrum, wind, blocks, winds, places, sem, wind_sem):
+    per_row = spectrum.shape[2] // LANES
+    count = blocks.shape[0]
+    lane = lax.broadcasted_iota(jnp.int32, (8, LANES), 1)
+    across = jnp.full((8, LANES), NO_ROW, jnp.int32)
+    down = []
+    copies = []
+    for q in range(count - 1):
+        place = lax.div(sea[0, q * LANES], LANES)
+        row = lax.div(place, per_row)
+        col = pl.multiple_of(lax.rem(place, per_row) * LANES, LANES)
+        copies.append(pltpu.make_async_copy(spectrum.at[:, row, pl.ds(col, LANES)], blocks.at[q], sem.at[q]))
+        copies.append(pltpu.make_async_copy(wind.at[:, row, pl.ds(col, LANES)], winds.at[q], wind_sem.at[q]))
+        copies[-2].start()
+        copies[-1].start()
+        across = jnp.where(lane == q, place, across)
+        places[8 + q:9 + q, :] = jnp.full((1, LANES), place, jnp.int32)
+    places[0:8, :] = across
+    places[7 + count:8 + count, :] = jnp.full((1, LANES), NO_COLUMN, jnp.int32)
+    blocks[count - 1] = jnp.zeros(blocks.shape[1:], blocks.dtype)
+    winds[count - 1] = jnp.zeros(winds.shape[1:], winds.dtype)
+    for copy in copies:
+        copy.wait()
+
+
+def relatives(s):
+    return (s + 1 - 2 * lax.rem(s, 2), lax.rem(s + 2, 4), 3 - s)
+
+
+def cuts(comps):
+    starts = list(range(0, comps - GROUP // 2, GROUP))
+    return list(zip(starts, starts[1:] + [comps]))
+
+
+def exchange_kernel(ends, per_row, span, blocks, winds, places, coef, trig_hbm, transfer_hbm, out, *scratch):
+    groups = cuts(blocks.shape[1])
+    fields = scratch[:len(groups)]
+    results = scratch[len(groups):2 * len(groups)]
+    (came, points, low, gamma, made, trig, transfer, bank, first, second, lists, found, table,
+     in_send, in_recv, out_send, out_recv, halo_send, halo_recv, own_sem, kept_sem,
+     list_send, list_recv, load_sem, result_sem) = scratch[2 * len(groups):]
+    s = lax.axis_index("spec")
+    z = lax.axis_index("space")
+    peers = relatives(s)
+    comps = blocks.shape[1]
+    count = blocks.shape[0]
+    chunks = count // 4
+    total = points.shape[0]
+
+    barrier = pltpu.get_barrier_semaphore()
+    for peer in peers:
+        pl.semaphore_signal(barrier, inc=1, device_id={"spec": peer}, device_id_type=MESH)
+
+    @pl.when(z > 0)
+    def _():
+        pl.semaphore_signal(barrier, inc=1, device_id={"space": z - 1}, device_id_type=MESH)
+
+    @pl.when(z < ends)
+    def _():
+        pl.semaphore_signal(barrier, inc=1, device_id={"space": z + 1}, device_id_type=MESH)
+
+    pl.semaphore_wait(barrier, 3 + jnp.minimum(z, 1) + jnp.minimum(ends - z, 1))
+
+    def inward(c, j, sending):
+        source = blocks.at[chunks * peers[j] + c]
+        target = came.at[c, s if sending else peers[j]]
+        return pltpu.make_async_remote_copy(
+            src_ref=source, dst_ref=target, send_sem=in_send.at[c, j], recv_sem=in_recv.at[c, j],
+            device_id={"spec": peers[j]}, device_id_type=MESH)
+
+    def outward(g, c, j, sending):
+        source = made.at[c, peers[j], pl.ds(groups[g][0], groups[g][1] - groups[g][0])]
+        target = fields[g].at[count + chunks * (s if sending else peers[j]) + c]
+        return pltpu.make_async_remote_copy(
+            src_ref=source, dst_ref=target, send_sem=out_send.at[g, c, j], recv_sem=out_recv.at[g, c, j],
+            device_id={"spec": peers[j]}, device_id_type=MESH)
+
+    def own(c):
+        return pltpu.make_async_copy(blocks.at[chunks * s + c], came.at[c, s], own_sem.at[c])
+
+    def kept(g, c):
+        source = made.at[c, s, pl.ds(groups[g][0], groups[g][1] - groups[g][0])]
+        return pltpu.make_async_copy(source, fields[g].at[count + chunks * s + c], kept_sem.at[g, c])
+
+    def halo(g, part, d, way):
+        return pltpu.make_async_remote_copy(
+            src_ref=fields[g].at[pl.ds(count + chunks * d, chunks)],
+            dst_ref=fields[g].at[pl.ds(2 * way * count + chunks * d, chunks)],
+            send_sem=halo_send.at[g, way, part], recv_sem=halo_recv.at[g, way, part],
+            device_id={"space": z + 1 - 2 * way}, device_id_type=MESH)
+
+    def listed(way):
+        return pltpu.make_async_remote_copy(
+            src_ref=places, dst_ref=lists.at[way], send_sem=list_send.at[way], recv_sem=list_recv.at[way],
+            device_id={"space": z + 1 - 2 * way}, device_id_type=MESH)
+
+    def result(g):
+        lo, hi = groups[g]
+        return pltpu.make_async_copy(results[g], out.at[:, pl.ds(lo, hi - lo)], result_sem.at[g])
+
+    loads = (pltpu.make_async_copy(trig_hbm, trig, load_sem.at[0]),
+             pltpu.make_async_copy(transfer_hbm, transfer, load_sem.at[1]))
+
+    for c in range(chunks):
+        own(c).start()
+        for j in (2, 0, 1):
+            inward(c, j, True).start()
+
+    for load in loads:
+        load.start()
+
+    @pl.when(z < ends)
+    def _():
+        listed(0).start()
+
+    @pl.when(z > 0)
+    def _():
+        listed(1).start()
+
+    @pl.when(z == 0)
+    def _():
+        for field in fields:
+            field[0:count] = jnp.zeros((count,) + field.shape[1:], field.dtype)
+
+    @pl.when(z == ends)
+    def _():
+        for field in fields:
+            field[2 * count:3 * count] = jnp.zeros((count,) + field.shape[1:], field.dtype)
+
+    wide = (comps, LANES)
+    cx = coef[:, 0:1]
+    cy = coef[:, 1:2]
+    bank[0] = jnp.broadcast_to(1.0 - jnp.abs(cx) - jnp.abs(cy), wide)
+    bank[1] = jnp.broadcast_to(jnp.maximum(cx, 0.0), wide)
+    bank[2] = jnp.broadcast_to(-jnp.minimum(cx, 0.0), wide)
+    bank[3] = jnp.broadcast_to(cy, wide)
+
+    @pl.when(z < ends)
+    def _():
+        listed(1).wait_recv()
+
+    @pl.when(z > 0)
+    def _():
+        listed(0).wait_recv()
+
+    slabs = []
+    for slab in range(3):
+        if slab == 1:
+            across, down = places[0:8, :], places[8:8 + count, :]
+        else:
+            there = z > 0 if slab == 0 else z < ends
+            side = lists[slab // 2]
+            across = jnp.where(there, side[0:8, :], NO_ROW)
+            down = jnp.where(there, side[8:8 + count, :], NO_COLUMN)
+        slabs.append((across, down + slab * span))
+    empty = 2 * count - 1
+    sub = lax.broadcasted_iota(jnp.int32, (count, LANES), 0)
+    for slab, (across, _) in enumerate(slabs):
+        place = across[0:1, :]
+        col = lax.rem(place, per_row)
+        base = place - col + slab * span
+        goals = (base + lax.rem(col + per_row - 1, per_row), base + lax.rem(col + 1, per_row),
+                 base + col - per_row, base + col + per_row)
+        for k, goal in enumerate(goals):
+            index = jnp.full((1, LANES), empty, jnp.int32)
+            for other, (_, down) in enumerate(slabs):
+                hit = jnp.where(down == goal, sub + (other * count - empty), 0)
+                index = index + jnp.sum(hit, axis=0, keepdims=True)
+            found[4 * slab + k:4 * slab + k + 1, :] = index
+    found[12:16, :] = jnp.full((4, LANES), empty, jnp.int32)
+    to_table = pltpu.make_async_copy(found, table, load_sem.at[2])
+    to_table.start()
+    to_table.wait()
+    for load in loads:
+        load.wait()
+
+    def chunk(c, carry):
+        own(c).wait()
+        for j in range(3):
+            inward(c, j, False).wait_recv()
+        for p in range(4):
+            points[p * comps:(p + 1) * comps, :] = came[c, p]
+        pair = winds[chunks * s + c]
+        drive = jnp.maximum(trig[:, 0:1] * pair[0:1, :] + trig[:, 1:2] * pair[1:2, :], 0.0)
+        gamma[...] = trig[:, 2:3] * drive
+
+        def source(step, carry):
+            e = points[...]
+            low[...] = e.astype(jnp.bfloat16)
+            mean = jnp.sum(e, axis=0, keepdims=True) * (1.0 / total)
+            moved = jnp.dot(transfer[...], low[...], preferred_element_type=jnp.float32)
+            points[...] = e + (gamma[...] - whitecap * mean) * e + moved
+            return carry
+
+        lax.fori_loop(0, SRC_STEPS, source, 0)
+        for p in range(4):
+            made[c, p] = points[p * comps:(p + 1) * comps, :]
+        for j in (2, 0, 1):
+            outward(0, c, j, True).start()
+        kept(0, c).start()
+        return carry
+
+    lax.fori_loop(0, chunks, chunk, 0)
+
+    for g in range(1, len(groups)):
+        def send(c, carry, g=g):
+            for j in (2, 0, 1):
+                outward(g, c, j, True).start()
+            kept(g, c).start()
+            return carry
+
+        lax.fori_loop(0, chunks, send, 0)
+
+    def send_halo(g):
+        def send(part, d):
+            @pl.when(z < ends)
+            def _():
+                halo(g, part, d, 0).start()
+
+            @pl.when(z > 0)
+            def _():
+                halo(g, part, d, 1).start()
+
+        for c in range(chunks):
+            kept(g, c).wait()
+        send(3, s)
+        for j in range(3):
+            for c in range(chunks):
+                outward(g, c, j, False).wait_recv()
+            send(j, peers[j])
+
+    def take_halo(g):
+        for part, d in enumerate(peers + (s,)):
+            @pl.when(z < ends)
+            def _():
+                halo(g, part, d, 1).wait_recv()
+
+            @pl.when(z > 0)
+            def _():
+                halo(g, part, d, 0).wait_recv()
+
+    def advance_group(g):
+        lo, hi = groups[g]
+        size = hi - lo
+        lane = lax.broadcasted_iota(jnp.int32, (size, LANES), 1)
+        for step, lead in enumerate((1, 3, 7, count)):
+            old = (fields[g], first, second, first)[step]
+            new = (first, second, first, results[g])[step]
+            last = 3 * count - 1 - lead if step < 3 else 2 * count - 1
+            shift = count if step == 3 else 0
+
+            def one(n, carry):
+                slab = lax.div(n, count)
+                q = lax.rem(n, count)
+                left = table[4 * slab, q]
+                right = table[4 * slab + 1, q]
+                upper = table[4 * slab + 2, q]
+                lower = table[4 * slab + 3, q]
+
+                def of(i):
+                    return old[i] if step == 0 else old[i, 0:size]
+
+                e = of(n)
+                to_right = pltpu.roll(jnp.where(lane == LANES - 1, of(left), e), 1, 1)
+                to_left = pltpu.roll(jnp.where(lane == 0, of(right), e), LANES - 1, 1)
+                cy = bank[3, lo:hi]
+                moved = (bank[0, lo:hi] * e + bank[1, lo:hi] * of(upper) + bank[2, lo:hi] * of(lower)
+                         + jnp.abs(cy) * jnp.where(cy > 0.0, to_right, to_left))
+                if step == 3:
+                    new[n - shift] = moved
+                else:
+                    new[n, 0:size] = moved
+                return carry
+
+            lax.fori_loop(lead, last + 1, one, 0)
+        result(g).start()
+
+    for g in range(len(groups)):
+        send_halo(g)
+        if g:
+            take_halo(g - 1)
+            advance_group(g - 1)
+    take_halo(len(groups) - 1)
+    advance_group(len(groups) - 1)
+
+    def finish(c, carry):
+        for j in range(3):
+            inward(c, j, True).wait_send()
+            for g in range(len(groups)):
+                outward(g, c, j, True).wait_send()
+        return carry
+
+    lax.fori_loop(0, chunks, finish, 0)
+    for way in range(2):
+        @pl.when(z < ends if way == 0 else z > 0)
+        def _():
+            listed(way).wait_send()
+            for g in range(len(groups)):
+                for part, d in enumerate(peers + (s,)):
+                    halo(g, part, d, way).wait_send()
+
+    for g in range(len(groups)):
+        result(g).wait()
+
+
+def expand_kernel(sea, blocks, out, table, sems):
+    count = blocks.shape[0]
+    rows, per_row = out.shape[1], out.shape[2] // LANES
+    for i in range(rows * per_row):
+        table[i] = count - 1
+    for q in range(count - 1):
+        table[lax.div(sea[0, q * LANES], LANES)] = q
+    copies = []
+    for i in range(rows * per_row):
+        row, col = divmod(i, per_row)
+        copies.append(pltpu.make_async_copy(
+            blocks.at[table[i]], out.at[:, row, col * LANES:(col + 1) * LANES], sems.at[i]))
+        copies[-1].start()
+    for copy in copies:
+        copy.wait()
+
+
+def fast_body(spectrum, wind, courant, transfer, sea_cells):
+    comps, rows, cols = spectrum.shape
+    total = transfer.shape[0]
+    count = sea_cells.shape[1] // LANES + 1
+    chunks = count // 4
+    ends = lax.axis_size("space") - 1
+    dma = pltpu.SemaphoreType.DMA
+    vmem = pl.BlockSpec(memory_space=pltpu.VMEM)
+    smem = pl.BlockSpec(memory_space=pltpu.SMEM)
+    hbm = pl.BlockSpec(memory_space=pl.ANY)
+    f32 = jnp.float32
+
+    blocks, winds, places = pl.pallas_call(
+        compact_kernel,
+        out_shape=(jax.ShapeDtypeStruct((count, comps, LANES), f32), jax.ShapeDtypeStruct((count, 2, LANES), f32),
+                   jax.ShapeDtypeStruct((8 + count, LANES), jnp.int32)),
+        in_specs=[smem, hbm, hbm],
+        out_specs=(vmem, vmem, vmem),
+        scratch_shapes=[dma((count,)), dma((count,))],
+        name="compact",
+    )(sea_cells, spectrum, wind)
+
+    angle = np.arange(NDIR, dtype=np.float32) * np.float32(2.0 * math.pi / NDIR)
+    growth = np.float32(growth_rate) * (np.arange(NFREQ, dtype=np.float32) + 1.0) / NFREQ
+    trig = jnp.asarray(np.stack([
+        np.repeat(np.cos(angle), NFREQ), np.repeat(np.sin(angle), NFREQ), np.tile(growth, NDIR)], axis=1), f32)
+
+    per_row = cols // LANES
+    parts = cuts(comps)
+    n = len(parts)
+    field = [pltpu.VMEM((3 * count, hi - lo, LANES), f32) for lo, hi in parts]
+    made = [pltpu.VMEM((count, hi - lo, LANES), f32) for lo, hi in parts]
+    most = max(hi - lo for lo, hi in parts)
+    moved = pl.pallas_call(
+        lambda *refs: exchange_kernel(ends, per_row, rows * per_row, *refs),
+        out_shape=jax.ShapeDtypeStruct((count, comps, LANES), f32),
+        in_specs=[vmem, vmem, vmem, vmem, hbm, hbm],
+        out_specs=hbm,
+        scratch_shapes=field + made + [
+            pltpu.VMEM((chunks, 4, comps, LANES), f32),
+            pltpu.VMEM((total, LANES), f32),
+            pltpu.VMEM((total, LANES), jnp.bfloat16),
+            pltpu.VMEM((total, LANES), f32),
+            pltpu.VMEM((chunks, 4, comps, LANES), f32),
+            pltpu.VMEM(trig.shape, f32),
+            pltpu.VMEM(transfer.shape, transfer.dtype),
+            pltpu.VMEM((4, comps, LANES), f32),
+            pltpu.VMEM((3 * count, most, LANES), f32),
+            pltpu.VMEM((3 * count, most, LANES), f32),
+            pltpu.VMEM((2, 8 + count, LANES), jnp.int32),
+            pltpu.VMEM((16, LANES), jnp.int32),
+            pltpu.SMEM((16, LANES), jnp.int32),
+            dma((chunks, 3)), dma((chunks, 3)), dma((n, chunks, 3)), dma((n, chunks, 3)),
+            dma((n, 2, 4)), dma((n, 2, 4)), dma((chunks,)), dma((n, chunks)),
+            dma((2,)), dma((2,)), dma((3,)), dma((n,)),
+        ],
+        compiler_params=pltpu.CompilerParams(collective_id=0, has_side_effects=True, vmem_limit_bytes=48 << 20),
+        name="exchange",
+    )(blocks, winds, places, courant.T, trig, transfer)
+
+    return pl.pallas_call(
+        expand_kernel,
+        out_shape=jax.ShapeDtypeStruct(spectrum.shape, f32),
+        in_specs=[smem, vmem],
+        out_specs=hbm,
+        scratch_shapes=[pltpu.SMEM((rows * per_row,), jnp.int32), dma((rows * per_row,))],
+        name="expand",
+    )(sea_cells, moved)
+
+
 def solution(mesh):
+    def step(*args):
+        if fits(mesh, *args):
+            return fast_body(*args)
+        return body(*args)
+
     in_specs = (
         P("spec", "space", None),
         P(None, "space", None),
@@ -98,4 +518,4 @@
         P("space", None),
     )
     out_specs = P("spec", "space", None)
-    return jax.shard_map(body, mesh=mesh, in_specs=in_specs, out_specs=out_specs, check_vma=False)
+    return jax.shard_map(step, mesh=mesh, in_specs=in_specs, out_specs=out_specs, check_vma=False)

time: 334 us -> 145 us (0.43); the launches traced: 329 us -> 145 us
  Pallas kernels: 0 us -> 141 us
  waiting for transfers between devices: 91.9 us -> 0 us
  local copies, waits for them, and re-layouts: 71.5 us -> 3.83 us
  blocking collectives: 62.8 us -> 0 us
  other arithmetic: 41 us -> 0 us
  starting transfers between devices: 32.9 us -> 0 us
  matrix products: 28.5 us -> 0 us
    pallas_call x0 -> x3, Pallas kernels: none -> 141 us  [the longest x1 132 us: fast_body(): pl.pallas_call(lambda *refs: exchange_kernel(ends, per_row, rows * per_ro...]
    all_to_all x1 -> x0, blocking collectives: 62.8 us -> none  [body(): lax.all_to_all(updated, 'spec', split_axis=0, concat_axis=1, tiled=True)]
    all_to_all x1 -> x0, waiting for transfers between devices: 59.6 us -> none  [body(): lax.all_to_all(masked, 'spec', split_axis=1, concat_axis=0, tiled=True)]
    slice x21 -> x0, local copies, waits for them, and re-layouts: 39 us -> none  [the longest x8 22.8 us: advance(): right = jnp.roll(centre, -1, axis=2)]
    mul x9 -> x0, other arithmetic: 37.2 us -> none  [the longest x4 29.2 us: body(): field = advance(padded, cx, cy) * mask_rows]
    ppermute x8 -> x0, waiting for transfers between devices: 32.3 us -> none  [the longest x4 23.5 us: padded_2(): lax.ppermute(head, axis, [((i + 1) % count, i) for i in range(ends)])]
    dot_general x4 -> x0, matrix products: 28.5 us -> none  [source_terms(): moved = jnp.dot(transfer, low, preferred_element_type=jnp.float32)]
    ppermute x8 -> x0, starting transfers between devices: 27.2 us -> none  [the longest x4 16.9 us: padded_2(): lax.ppermute(tail, axis, [(i, (i + 1) % count) for i in range(ends)])]
  transfers between devices with their start and end apart: 9 -> 0, of which waited for: 9 -> 0; matrix products, arithmetic and copies ran while one was open for 11% -> 0% of each run, Pallas kernels for 0% -> 0%
where the time goes in v2:
time: 145 us
  Pallas kernels  141 us (97%)
  local copies, waits for them, and re-layouts  3.83 us (3%)
    pallas_call x1, Pallas kernels, fast_body(): pl.pallas_call(lambda *refs: exchange_kernel(ends, per_row, rows * per_ro...  132 us
    pallas_call x1, Pallas kernels, fast_body(): pl.pallas_call(compact_kernel, out_shape=(jax.ShapeDtypeStruct((count, co...  4.7 us
    pallas_call x1, Pallas kernels, fast_body(): pl.pallas_call(expand_kernel, out_shape=jax.ShapeDtypeStruct(spectrum.sha...  4.43 us
    unnamed x9, local copies, waits for them, and re-layouts  3.83 us

profile of v2, /device:TPU:1, one launch (start us, length us, event | category | flops | bytes accessed | tf_op | source)
XLA Modules:
  0.0 144.8 jit_solution(8928708582754367410)
XLA Ops:
  0.0 0.0 copy-start.1
  0.0 0.9 copy.7
  0.9 4.7 %compact.1 = (f32[16,324,128]{2,1,0:T(8,128)}, f32[16,2,128]{2,1,0:T(2,128)}, s32[24,128]{1,0:T(8,128)}) custom-call(s32[1,1920]{1,0:T(1,128)} %sea.3, f32[324,4,1024]{2,1,0:T(4,128)} %spectrum.1, f32[2,4,1024]{2,1,0:T(4,128)} %wind.1), custom_call_target="tpu_custom_call" | custom-call | tf_op jit(solution)/shard_map/compact/pallas_call | solution.py:449
  5.6 0.0 copy-done.1
  5.6 0.0 copy-start.2
  5.6 0.7 copy-done.2
  6.3 0.0 copy-start.3
  6.3 0.7 copy-done.3
  7.0 131.8 %exchange.1.blocks = f32[16,324,128]{2,1,0:T(8,128)S(1)} custom-call(f32[16,324,128]{2,1,0:T(8,128)} %get-tuple-element.8.refs_0_, f32[16,2,128]{2,1,0:T(2,128)S(1)} %copy-done.2, s32[24,128]{1,0:T(8,128)S(1)} %copy-done.3, f32[324,2]{1,0:T(8,128)S(1)} %bitcast.1, f32[1296,3]{1,0:T(8,128)S(1)} %copy-done.1, bf16[1296,1296]{1,0:T(8,128)(2,1)} %refs_5_.1), custom_call_target="tpu_custom_call" | custom-call | tf_op jit(solution)/shard_map/exchange/pallas_call | solution.py:470
  138.9 0.0 copy-start
  138.9 1.5 %copy-done = f32[16,324,128]{2,1,0:T(8,128)} copy-done((f32[16,324,128]{2,1,0:T(8,128)}, f32[16,324,128]{2,1,0:T(8,128)S(1)}, u32[]{:S(2)}) %copy-start) | copy-done | bytes 2654232
  140.4 4.4 %expand.1 = f32[324,4,1024]{2,1,0:T(4,128)} custom-call(s32[1,1920]{1,0:T(1,128)} %sea.3, f32[16,324,128]{2,1,0:T(8,128)} %copy-done), custom_call_target="tpu_custom_call" | custom-call | tf_op jit(solution)/shard_map/expand/pallas_call | solution.py:497
Async XLA Ops:
  0.0 5.6 %copy-start.1 = (f32[1296,3]{1,0:T(8,128)S(1)}, f32[1296,3]{1,0:T(8,128)}, u32[]{:S(2)}) copy-start(f32[1296,3]{1,0:T(8,128)} %constant.2.clone.refs_4_) | copy-start | bytes 46660
  5.6 0.7 copy-start.2
  6.3 0.7 copy-start.3
  138.9 1.5 %copy-start = (f32[16,324,128]{2,1,0:T(8,128)}, f32[16,324,128]{2,1,0:T(8,128)S(1)}, u32[]{:S(2)}) copy-start(f32[16,324,128]{2,1,0:T(8,128)S(1)} %exchange.1.blocks) | copy-start | bytes 7962628

commit v3 on v2

--- a/solution.py
+++ b/solution.py
@@ -95,6 +95,7 @@
 LANES = 128
 NO_ROW = -5000
 NO_COLUMN = -1000
+AT_ONCE = 4
 GROUP = 56
 MESH = pl.DeviceIdType.MESH
 
@@ -146,11 +147,11 @@
     return list(zip(starts, starts[1:] + [comps]))
 
 
-def exchange_kernel(ends, per_row, span, blocks, winds, places, coef, trig_hbm, transfer_hbm, out, *scratch):
+def exchange_kernel(ends, per_row, span, blocks, winds_hbm, places_hbm, coef_hbm, trig_hbm, transfer_hbm, out, *scratch):
     groups = cuts(blocks.shape[1])
     fields = scratch[:len(groups)]
     results = scratch[len(groups):2 * len(groups)]
-    (came, points, low, gamma, made, trig, transfer, bank, first, second, lists, found, table,
+    (came, points, low, gamma, made, trig, transfer, winds, places, coef, bank, first, second, lists, found, table,
      in_send, in_recv, out_send, out_recv, halo_send, halo_recv, own_sem, kept_sem,
      list_send, list_recv, load_sem, result_sem) = scratch[2 * len(groups):]
     s = lax.axis_index("spec")
@@ -205,32 +206,33 @@
 
     def listed(way):
         return pltpu.make_async_remote_copy(
-            src_ref=places, dst_ref=lists.at[way], send_sem=list_send.at[way], recv_sem=list_recv.at[way],
+            src_ref=places_hbm, dst_ref=lists.at[way], send_sem=list_send.at[way], recv_sem=list_recv.at[way],
             device_id={"space": z + 1 - 2 * way}, device_id_type=MESH)
 
     def result(g):
         lo, hi = groups[g]
         return pltpu.make_async_copy(results[g], out.at[:, pl.ds(lo, hi - lo)], result_sem.at[g])
 
-    loads = (pltpu.make_async_copy(trig_hbm, trig, load_sem.at[0]),
-             pltpu.make_async_copy(transfer_hbm, transfer, load_sem.at[1]))
-
+    loads = [pltpu.make_async_copy(source, target, load_sem.at[i]) for i, (source, target) in enumerate((
+        (places_hbm, places), (coef_hbm, coef), (winds_hbm, winds), (trig_hbm, trig), (transfer_hbm, transfer)))]
+
+    @pl.when(z < ends)
+    def _():
+        listed(0).start()
+
+    @pl.when(z > 0)
+    def _():
+        listed(1).start()
+
+    for c in range(chunks):
+        for j in (2, 0, 1):
+            inward(c, j, True).start()
     for c in range(chunks):
         own(c).start()
-        for j in (2, 0, 1):
-            inward(c, j, True).start()
 
     for load in loads:
         load.start()
 
-    @pl.when(z < ends)
-    def _():
-        listed(0).start()
-
-    @pl.when(z > 0)
-    def _():
-        listed(1).start()
-
     @pl.when(z == 0)
     def _():
         for field in fields:
@@ -242,12 +244,14 @@
             field[2 * count:3 * count] = jnp.zeros((count,) + field.shape[1:], field.dtype)
 
     wide = (comps, LANES)
-    cx = coef[:, 0:1]
-    cy = coef[:, 1:2]
-    bank[0] = jnp.broadcast_to(1.0 - jnp.abs(cx) - jnp.abs(cy), wide)
-    bank[1] = jnp.broadcast_to(jnp.maximum(cx, 0.0), wide)
-    bank[2] = jnp.broadcast_to(-jnp.minimum(cx, 0.0), wide)
-    bank[3] = jnp.broadcast_to(cy, wide)
+    loads[0].wait()
+    loads[1].wait()
+    cx = jnp.broadcast_to(coef[0:1, :], wide[::-1]).T
+    cy = jnp.broadcast_to(coef[1:2, :], wide[::-1]).T
+    bank[0] = 1.0 - jnp.abs(cx) - jnp.abs(cy)
+    bank[1] = jnp.maximum(cx, 0.0)
+    bank[2] = -jnp.minimum(cx, 0.0)
+    bank[3] = cy
 
     @pl.when(z < ends)
     def _():
@@ -269,6 +273,8 @@
         slabs.append((across, down + slab * span))
     empty = 2 * count - 1
     sub = lax.broadcasted_iota(jnp.int32, (count, LANES), 0)
+    at = lax.div(lax.broadcasted_iota(jnp.int32, (1, LANES), 1), count)
+    tables = [jnp.full((1, LANES), empty, jnp.int32)] * 4
     for slab, (across, _) in enumerate(slabs):
         place = across[0:1, :]
         col = lax.rem(place, per_row)
@@ -280,12 +286,15 @@
             for other, (_, down) in enumerate(slabs):
                 hit = jnp.where(down == goal, sub + (other * count - empty), 0)
                 index = index + jnp.sum(hit, axis=0, keepdims=True)
-            found[4 * slab + k:4 * slab + k + 1, :] = index
-    found[12:16, :] = jnp.full((4, LANES), empty, jnp.int32)
-    to_table = pltpu.make_async_copy(found, table, load_sem.at[2])
+            moved = pltpu.roll(jnp.broadcast_to(index, (8, LANES)), slab * count, 1)[0:1, :] if slab else index
+            tables[k] = jnp.where(at == slab, moved, tables[k])
+    for k in range(4):
+        found[k:k + 1, :] = tables[k]
+    found[4:8, :] = jnp.full((4, LANES), empty, jnp.int32)
+    to_table = pltpu.make_async_copy(found, table, load_sem.at[5])
     to_table.start()
     to_table.wait()
-    for load in loads:
+    for load in loads[2:]:
         load.wait()
 
     def chunk(c, carry):
@@ -360,33 +369,32 @@
         for step, lead in enumerate((1, 3, 7, count)):
             old = (fields[g], first, second, first)[step]
             new = (first, second, first, results[g])[step]
-            last = 3 * count - 1 - lead if step < 3 else 2 * count - 1
-            shift = count if step == 3 else 0
-
-            def one(n, carry):
-                slab = lax.div(n, count)
-                q = lax.rem(n, count)
-                left = table[4 * slab, q]
-                right = table[4 * slab + 1, q]
-                upper = table[4 * slab + 2, q]
-                lower = table[4 * slab + 3, q]
-
+            due = 3 * count - 2 * lead if step < 3 else count
+            trips = -(-due // AT_ONCE)
+            start = (3 * count - trips * AT_ONCE) // 2
+
+            def some(trip, carry):
                 def of(i):
                     return old[i] if step == 0 else old[i, 0:size]
 
-                e = of(n)
-                to_right = pltpu.roll(jnp.where(lane == LANES - 1, of(left), e), 1, 1)
-                to_left = pltpu.roll(jnp.where(lane == 0, of(right), e), LANES - 1, 1)
                 cy = bank[3, lo:hi]
-                moved = (bank[0, lo:hi] * e + bank[1, lo:hi] * of(upper) + bank[2, lo:hi] * of(lower)
-                         + jnp.abs(cy) * jnp.where(cy > 0.0, to_right, to_left))
-                if step == 3:
-                    new[n - shift] = moved
-                else:
-                    new[n, 0:size] = moved
+                results_here = []
+                for k in range(AT_ONCE):
+                    n = start + trip * AT_ONCE + k
+                    e = of(n)
+                    to_right = pltpu.roll(jnp.where(lane == LANES - 1, of(table[0, n]), e), 1, 1)
+                    to_left = pltpu.roll(jnp.where(lane == 0, of(table[1, n]), e), LANES - 1, 1)
+                    results_here.append(
+                        (n, bank[0, lo:hi] * e + bank[1, lo:hi] * of(table[2, n]) + bank[2, lo:hi] * of(table[3, n])
+                         + jnp.abs(cy) * jnp.where(cy > 0.0, to_right, to_left)))
+                for n, moved in results_here:
+                    if step == 3:
+                        new[n - count] = moved
+                    else:
+                        new[n, 0:size] = moved
                 return carry
 
-            lax.fori_loop(lead, last + 1, one, 0)
+            lax.fori_loop(0, trips, some, 0)
         result(g).start()
 
     for g in range(len(groups)):
@@ -470,7 +478,7 @@
     moved = pl.pallas_call(
         lambda *refs: exchange_kernel(ends, per_row, rows * per_row, *refs),
         out_shape=jax.ShapeDtypeStruct((count, comps, LANES), f32),
-        in_specs=[vmem, vmem, vmem, vmem, hbm, hbm],
+        in_specs=[hbm] * 6,
         out_specs=hbm,
         scratch_shapes=field + made + [
             pltpu.VMEM((chunks, 4, comps, LANES), f32),
@@ -480,19 +488,22 @@
             pltpu.VMEM((chunks, 4, comps, LANES), f32),
             pltpu.VMEM(trig.shape, f32),
             pltpu.VMEM(transfer.shape, transfer.dtype),
+            pltpu.VMEM((count, 2, LANES), f32),
+            pltpu.VMEM((8 + count, LANES), jnp.int32),
+            pltpu.VMEM(courant.shape, f32),
             pltpu.VMEM((4, comps, LANES), f32),
             pltpu.VMEM((3 * count, most, LANES), f32),
             pltpu.VMEM((3 * count, most, LANES), f32),
             pltpu.VMEM((2, 8 + count, LANES), jnp.int32),
-            pltpu.VMEM((16, LANES), jnp.int32),
-            pltpu.SMEM((16, LANES), jnp.int32),
+            pltpu.VMEM((8, LANES), jnp.int32),
+            pltpu.SMEM((8, LANES), jnp.int32),
             dma((chunks, 3)), dma((chunks, 3)), dma((n, chunks, 3)), dma((n, chunks, 3)),
             dma((n, 2, 4)), dma((n, 2, 4)), dma((chunks,)), dma((n, chunks)),
-            dma((2,)), dma((2,)), dma((3,)), dma((n,)),
+            dma((2,)), dma((2,)), dma((6,)), dma((n,)),
         ],
-        compiler_params=pltpu.CompilerParams(collective_id=0, has_side_effects=True, vmem_limit_bytes=48 << 20),
+        compiler_params=pltpu.CompilerParams(collective_id=0, has_side_effects=True, vmem_limit_bytes=67043328),
         name="exchange",
-    )(blocks, winds, places, courant.T, trig, transfer)
+    )(blocks, winds, places, courant, trig, transfer)
 
     return pl.pallas_call(
         expand_kernel,

time: 145 us -> 98.7 us (0.68)
  Pallas kernels: 141 us -> 98.4 us
  local copies, waits for them, and re-layouts: 3.83 us -> 0 us
    pallas_call x1, Pallas kernels: 132 us -> 89.2 us  [fast_body(): pl.pallas_call(lambda *refs: exchange_kernel(ends, per_row, rows * per_ro...]
    unnamed x9 -> x0, local copies, waits for them, and re-layouts: 3.83 us -> none
where the time goes in v3:
time: 98.7 us; the launch traced here: 98.4 us
  Pallas kernels  98.4 us (100%)
    pallas_call x1, Pallas kernels, fast_body(): pl.pallas_call(lambda *refs: exchange_kernel(ends, per_row, rows * per_ro...  89.2 us
    pallas_call x1, Pallas kernels, fast_body(): pl.pallas_call(compact_kernel, out_shape=(jax.ShapeDtypeStruct((count, co...  4.7 us
    pallas_call x1, Pallas kernels, fast_body(): pl.pallas_call(expand_kernel, out_shape=jax.ShapeDtypeStruct(spectrum.sha...  4.43 us

profile of v3, /device:TPU:1, one launch (start us, length us, event | category | flops | bytes accessed | tf_op | source)
XLA Modules:
  0.0 98.4 jit_solution(8917499486864110493)
XLA Ops:
  0.0 4.7 %compact.1 = (f32[16,324,128]{2,1,0:T(8,128)}, f32[16,2,128]{2,1,0:T(2,128)}, s32[24,128]{1,0:T(8,128)}) custom-call(s32[1,1920]{1,0:T(1,128)} %sea.3, f32[324,4,1024]{2,1,0:T(4,128)} %spectrum.1, f32[2,4,1024]{2,1,0:T(4,128)} %wind.1), custom_call_target="tpu_custom_call" | custom-call | tf_op jit(solution)/shard_map/compact/pallas_call | solution.py:457
  4.7 89.2 %exchange.1.blocks = f32[16,324,128]{2,1,0:T(8,128)} custom-call(f32[16,324,128]{2,1,0:T(8,128)} %get-tuple-element.8.refs_0_, f32[16,2,128]{2,1,0:T(2,128)} %get-tuple-element.9.refs_1_, s32[24,128]{1,0:T(8,128)} %get-tuple-element.10.refs_2_, f32[2,324]{1,0:T(2,128)} %refs_3_.1, f32[1296,3]{1,0:T(8,128)} %constant.2.clone.refs_4_, bf16[1296,1296]{1,0:T(8,128)(2,1)} %refs_5_.1), custom_call_target="tpu_custom_call" | custom-call | tf_op jit(solution)/shard_map/exchange/pallas_call | solution.py:478
  94.0 4.4 %expand.1 = f32[324,4,1024]{2,1,0:T(4,128)} custom-call(s32[1,1920]{1,0:T(1,128)} %sea.3, f32[16,324,128]{2,1,0:T(8,128)} %exchange.1.blocks), custom_call_target="tpu_custom_call" | custom-call | tf_op jit(solution)/shard_map/expand/pallas_call | solution.py:508

commit v4 on v3

--- a/solution.py
+++ b/solution.py
@@ -96,7 +96,7 @@
 NO_ROW = -5000
 NO_COLUMN = -1000
 AT_ONCE = 4
-GROUP = 56
+SHARES = (0.0, 0.22, 0.42, 0.62, 0.79, 0.91)
 MESH = pl.DeviceIdType.MESH
 
 
@@ -143,7 +143,7 @@
 
 
 def cuts(comps):
-    starts = list(range(0, comps - GROUP // 2, GROUP))
+    starts = sorted({8 * round(comps * share / 8) for share in SHARES})
     return list(zip(starts, starts[1:] + [comps]))
 
 
@@ -399,11 +399,12 @@
 
     for g in range(len(groups)):
         send_halo(g)
-        if g:
-            take_halo(g - 1)
-            advance_group(g - 1)
-    take_halo(len(groups) - 1)
-    advance_group(len(groups) - 1)
+        if g >= 2:
+            take_halo(g - 2)
+            advance_group(g - 2)
+    for g in range(max(len(groups) - 2, 0), len(groups)):
+        take_halo(g)
+        advance_group(g)
 
     def finish(c, carry):
         for j in range(3):

time: 98.7 us -> 100 us (1.013)
  the two profiles are of different devices: /device:TPU:1 before, /device:TPU:0 now
where the time goes in v4:
time: 100 us; the launch traced here: 99.8 us
  Pallas kernels  99.8 us (100%)
    pallas_call x1, Pallas kernels, fast_body(): pl.pallas_call(lambda *refs: exchange_kernel(ends, per_row, rows * per_ro...  90.7 us
    pallas_call x1, Pallas kernels, fast_body(): pl.pallas_call(compact_kernel, out_shape=(jax.ShapeDtypeStruct((count, co...  4.7 us
    pallas_call x1, Pallas kernels, fast_body(): pl.pallas_call(expand_kernel, out_shape=jax.ShapeDtypeStruct(spectrum.sha...  4.43 us

profile of v4, /device:TPU:0, one launch (start us, length us, event | category | flops | bytes accessed | tf_op | source)
XLA Modules:
  0.0 99.8 jit_solution(9425795573873948048)
XLA Ops:
  0.0 4.7 %compact.1 = (f32[16,324,128]{2,1,0:T(8,128)}, f32[16,2,128]{2,1,0:T(2,128)}, s32[24,128]{1,0:T(8,128)}) custom-call(s32[1,1920]{1,0:T(1,128)} %sea.3, f32[324,4,1024]{2,1,0:T(4,128)} %spectrum.1, f32[2,4,1024]{2,1,0:T(4,128)} %wind.1), custom_call_target="tpu_custom_call" | custom-call | tf_op jit(solution)/shard_map/compact/pallas_call | solution.py:458
  4.7 90.7 %exchange.1.blocks = f32[16,324,128]{2,1,0:T(8,128)} custom-call(f32[16,324,128]{2,1,0:T(8,128)} %get-tuple-element.8.refs_0_, f32[16,2,128]{2,1,0:T(2,128)} %get-tuple-element.9.refs_1_, s32[24,128]{1,0:T(8,128)} %get-tuple-element.10.refs_2_, f32[2,324]{1,0:T(2,128)} %refs_3_.1, f32[1296,3]{1,0:T(8,128)} %constant.2.clone.refs_4_, bf16[1296,1296]{1,0:T(8,128)(2,1)} %refs_5_.1), custom_call_target="tpu_custom_call" | custom-call | tf_op jit(solution)/shard_map/exchange/pallas_call | solution.py:479
  95.4 4.4 %expand.1 = f32[324,4,1024]{2,1,0:T(4,128)} custom-call(s32[1,1920]{1,0:T(1,128)} %sea.3, f32[16,324,128]{2,1,0:T(8,128)} %exchange.1.blocks), custom_call_target="tpu_custom_call" | custom-call | tf_op jit(solution)/shard_map/expand/pallas_call | solution.py:509
